TPU v7x, 512 devices: a whole 4x8x8 slice. The times are simulated.
512 devices in a mesh: section: 8 (over x, core), expert: 64 (over z, y).
Axes of the slice: x: 4, y: 8, z: 8, core: 2. Of those that a mesh axis runs over, the one named last changes fastest.
Arguments:
- histories: bfloat16 [8, 8192, 5120], P('section', 'expert'), may hold values from -6 to 6
- page_map: int32 [8, 2, 2048], P('section', None, 'expert'), may hold values from 0 to 2047, as said below
- user_pages: int32 [8, 64, 4], P('section', 'expert'), may hold values from 1 to 16, 32 in all within a row
- tails: int32 [8, 64, 4], P('section', 'expert'), may hold values from 1 to 4
- routes: int32 [8, 8192, 2], P('section', 'expert'), may hold values from 0 to 31, all different within a row; in each aligned block of 128 rows (0 to 127, 128 to 255, ..., all dimensions but the last counted through in order) at most 16 rows name the same one
- out_proj: bfloat16 [8, 1024, 1024], P('section', 'expert'), may hold values from -0.1875 to 0.1875
- router: bfloat16 [8, 1024, 32], P('section'), may hold values from -0.75 to 0.75
- w_gate: bfloat16 [8, 1024, 32768], P('section', None, 'expert'), may hold values from -0.1875 to 0.1875
- w_up: bfloat16 [8, 1024, 32768], P('section', None, 'expert'), may hold values from -0.1875 to 0.1875
- w_down: bfloat16 [8, 32768, 1024], P('section', 'expert'), may hold values from -0.1875 to 0.1875
Outputs:
- handed: bfloat16 [8, 8192, 1024], P('section', 'expert')
Inputs may be any that keep to these rules, and one draw needn't show every extreme that they name: page_map[0] is a permutation of the pages of a section and page_map[1] its inverse; every device holds exactly 32 pages before and after; no device's pages send more than 1 pages to one device, and some send exactly 1. `user_pages`: the 4 entries of one device sum to 32, and the largest is 16. `routes`: A row names 2 different experts; among the rows of one device, no expert is named more than 16 times, a bound that some block reaches.
All inputs are finite; a program needn't handle non-finite values.
Results may differ from a plain program's by a relative error of at most 0.012.
Values may be sent and summed in bfloat16 or wider, within the bound.
No kernel may reach another device: no remote copies, remote signals or barrier semaphores. Data moves between devices by JAX's collectives and lax.ppermute only.
A program may use at most 64 MiB of HBM per device.

v0:
```python
import jax
import jax.numpy as jnp
from jax import lax
from jax.sharding import PartitionSpec as P

HEADS = 8


def swapped(shard, axis, apart):
    return lax.ppermute(shard, axis, [(i, i ^ 1 << apart) for i in range(lax.axis_size(axis))])


def from_behind(block, axis, distance):
    devices = range(lax.axis_size(axis))
    route = [((i - distance) % len(devices), i) for i in devices]
    return lax.ppermute(block, axis, route)


def layout_rows(counts, tail_rows, page_rows, row_count):
    starting = jnp.cumsum(counts) - counts
    length = (counts - 1) * page_rows + tail_rows
    row_index = jnp.arange(row_count, dtype=jnp.int32)
    page_of = row_index // page_rows
    owner_of = jnp.sum((starting[None, :] <= page_of[:, None]).astype(jnp.int32), axis=1) - 1
    member = owner_of[:, None] == jnp.arange(counts.shape[0], dtype=jnp.int32)[None, :]
    offset = jnp.sum(jnp.where(member, starting[None, :] * page_rows, 0), axis=1)
    spread = jnp.sum(jnp.where(member, length[None, :], 0), axis=1)
    return (owner_of, row_index - offset, spread)


def attend(balanced, counts, tail_rows, page_rows):
    row_count = balanced.shape[0]
    model_width = balanced.shape[1] // 5
    head_dim = model_width // HEADS
    owner_of, position, spread = layout_rows(counts, tail_rows, page_rows, row_count)
    allowed = (
        (owner_of[:, None] == owner_of[None, :])
        & (position[None, :] <= position[:, None])
        & (position[None, :] < spread[None, :])
    )
    queries = balanced[:, :model_width].reshape(row_count, HEADS, head_dim)
    key_rows = balanced[:, model_width : 2 * model_width].reshape(row_count, HEADS, head_dim)
    values = balanced[:, 2 * model_width : 3 * model_width].reshape(row_count, HEADS, head_dim)
    scores = jnp.einsum(
        "qhd,khd->hqk", queries, key_rows, preferred_element_type=jnp.float32
    ) * head_dim ** (-0.5)
    weights = (
        jnp.where(allowed[None], jax.nn.silu(scores), 0.0)
        / spread.astype(jnp.float32)[None, :, None]
    )
    weights = weights.astype(jnp.bfloat16)
    attended = jnp.einsum(
        "hqk,khd->qhd", weights, values, preferred_element_type=jnp.float32
    ).reshape(row_count, model_width)
    average = jnp.mean(attended, axis=1, keepdims=True)
    centered = attended - average
    variance = jnp.mean(centered * centered, axis=1, keepdims=True)
    gating = balanced[:, 3 * model_width : 4 * model_width].astype(jnp.float32)
    return (centered * lax.rsqrt(variance + 1e-05) * gating).astype(jnp.bfloat16)


def gate_share(normed, router, routes):
    logits = jnp.dot(normed, router, preferred_element_type=jnp.float32)
    scores = jax.nn.sigmoid(logits)
    picked = routes[:, :, None] == jnp.arange(router.shape[1], dtype=jnp.int32)[None, None, :]
    chosen = jnp.sum(jnp.where(picked, scores[:, None, :], 0.0), axis=2)
    return chosen / jnp.sum(chosen, axis=1, keepdims=True)


def slot_table(routes, experts, capacity):
    pair_count = routes.shape[0] * routes.shape[1]
    chosen = routes.reshape(-1)
    onehot = (chosen[:, None] == jnp.arange(experts, dtype=jnp.int32)[None, :]).astype(jnp.int32)
    before = jnp.cumsum(onehot, axis=0) - onehot
    ranking = jnp.sum(before * onehot, axis=1)
    slot_of_pair = chosen * capacity + ranking
    matches = slot_of_pair[None, :] == jnp.arange(experts * capacity, dtype=jnp.int32)[:, None]
    source_token = (
        jnp.sum(jnp.where(matches, jnp.arange(pair_count, dtype=jnp.int32)[None, :], 0), axis=1)
        // 2
    )
    return (slot_of_pair, source_token)


def whole_expert(incoming, gate_full, up_full, down_full):
    flat_rows = incoming.reshape(-1, incoming.shape[-1])
    gate_act = jnp.dot(flat_rows, gate_full, preferred_element_type=jnp.float32)
    up_act = jnp.dot(flat_rows, up_full, preferred_element_type=jnp.float32)
    hidden = (jax.nn.silu(gate_act) * up_act).astype(jnp.bfloat16)
    half_units = gate_full.shape[1] // 2
    first_part = jnp.dot(
        hidden[:, :half_units], down_full[:half_units], preferred_element_type=jnp.float32
    ).astype(jnp.bfloat16)
    second_part = jnp.dot(
        hidden[:, half_units:], down_full[half_units:], preferred_element_type=jnp.float32
    ).astype(jnp.bfloat16)
    summed = (first_part.astype(jnp.float32) + second_part.astype(jnp.float32)).astype(jnp.bfloat16)
    return summed.reshape(incoming.shape)


def shards(histories, page_map, user_pages, tails, routes, out_proj, router, w_gate, w_up, w_down):
    devices = lax.axis_size("expert")
    parity = lax.axis_index("expert") % 2
    row_count = histories.shape[1]
    stacked_width = histories.shape[2]
    model_width = stacked_width // 5
    pages_dev = page_map.shape[2]
    page_rows = row_count // pages_dev
    page_slots = (pages_dev + devices - 1) // devices
    page_block = histories[0].reshape(pages_dev, page_rows, stacked_width)
    target = page_map[0, 0]
    target_dev = target // pages_dev
    earlier = (target_dev[None, :] == target_dev[:, None]) & (target[None, :] < target[:, None])
    position = target_dev * page_slots + jnp.sum(earlier.astype(jnp.int32), axis=1)
    matches = position[None, :] == jnp.arange(devices * page_slots, dtype=jnp.int32)[:, None]
    chosen_page = jnp.sum(
        jnp.where(matches, jnp.arange(pages_dev, dtype=jnp.int32)[None, :], 0), axis=1
    )
    outgoing = page_block[chosen_page]
    arrived = lax.all_to_all(outgoing, "expert", split_axis=0, concat_axis=0, tiled=True)
    anchor = page_map[0, 1]
    anchor_dev = anchor // pages_dev
    ordering = jnp.arange(pages_dev, dtype=jnp.int32)
    sooner = (anchor_dev[None, :] == anchor_dev[:, None]) & (ordering[None, :] < ordering[:, None])
    where_from = anchor_dev * page_slots + jnp.sum(sooner.astype(jnp.int32), axis=1)
    balanced = arrived[where_from].reshape(row_count, stacked_width)
    mixed_in = attend(balanced, user_pages[0, 0], tails[0, 0], page_rows)
    projected = jnp.dot(
        mixed_in,
        lax.all_gather(out_proj, "expert", axis=1, tiled=True)[0],
        preferred_element_type=jnp.float32,
    )
    resid = (balanced[:, 4 * model_width :].astype(jnp.float32) + projected).astype(jnp.bfloat16)
    resid_wide = resid.astype(jnp.float32)
    normed = (
        resid_wide * lax.rsqrt(jnp.mean(resid_wide * resid_wide, axis=1, keepdims=True) + 1e-06)
    ).astype(jnp.bfloat16)
    experts = router.shape[2]
    capacity = 4 * row_count // experts
    share = gate_share(normed, router[0], routes[0])
    slot_of_pair, source_token = slot_table(routes[0], experts, capacity)
    packed = normed[source_token].reshape(experts, capacity, model_width)
    is_odd = parity == 1
    half_units = w_gate.shape[2]
    gate_up = jnp.concatenate([w_gate[0], w_up[0]], axis=1)
    other_gate_up = swapped(gate_up, "expert", 0)
    other_down = swapped(w_down[0], "expert", 0)
    own_gate = gate_up[:, :half_units]
    own_up = gate_up[:, half_units:]
    other_gate = other_gate_up[:, :half_units]
    other_up = other_gate_up[:, half_units:]
    gate_full = jnp.where(
        is_odd,
        jnp.concatenate([other_gate, own_gate], axis=1),
        jnp.concatenate([own_gate, other_gate], axis=1),
    )
    up_full = jnp.where(
        is_odd,
        jnp.concatenate([other_up, own_up], axis=1),
        jnp.concatenate([own_up, other_up], axis=1),
    )
    down_full = jnp.where(
        is_odd,
        jnp.concatenate([other_down, w_down[0]], axis=0),
        jnp.concatenate([w_down[0], other_down], axis=0),
    )
    half_cap = capacity // 2
    sent_rows = packed.reshape(experts * 2, half_cap, model_width)
    own_rows = lax.all_to_all(sent_rows, "expert", split_axis=0, concat_axis=0, tiled=True)
    served = whole_expert(own_rows, gate_full, up_full, down_full)
    came_back = lax.all_to_all(served, "expert", split_axis=0, concat_axis=0, tiled=True)
    result = came_back.reshape(experts, capacity, model_width)
    picked = result.reshape(experts * capacity, model_width)[slot_of_pair]
    picked = picked.reshape(row_count, 2, model_width).astype(jnp.float32)
    mixture = jnp.sum(picked * share[:, :, None], axis=1)
    output_rows = (resid_wide + mixture).astype(jnp.bfloat16)
    return from_behind(output_rows[None], "section", 1)


def solution(mesh):
    in_specs = (
        P("section", "expert", None),
        P("section", None, "expert"),
        P("section", "expert", None),
        P("section", "expert", None),
        P("section", "expert", None),
        P("section", "expert", None),
        P("section", None, None),
        P("section", None, "expert"),
        P("section", None, "expert"),
        P("section", "expert", None),
    )
    out_specs = P("section", "expert", None)
    return jax.shard_map(shards, mesh=mesh, in_specs=in_specs, out_specs=out_specs, check_vma=False)
```

profile of v0, /device:TPU:8, one launch (start us, length us, event | category | flops | bytes accessed | tf_op | source)
XLA Modules:
  0.0 289.1 jit_solution(12892616485323434839)
XLA Ops:
  6.5 0.8 and_select_fusion.2
  7.3 0.7 slice_bitcast_fusion
  8.3 2.6 reshape_squeeze.6
  10.9 4.2 %gather_fusion = bf16[64,4,5120]{2,1,0:T(4,128)(2,1)} fusion(bf16[32,4,5120]{2,1,0:T(4,128)(2,1)S(1)} %reshape_squeeze.6, s32[1024]{0:T(1024)S(1)} %pad_clamp_fusion.3), kind=kCustom, calls=%fused_computation | custom fusion | bytes 5243136 | tf_op jit(solution)/shard_map/gather | solution.py:119
  15.1 16.6 %all-to-all-start = ((bf16[64,4,5120]{2,1,0:T(4,128)(2,1)}), bf16[64,4,5120]{2,1,0:T(4,128)(2,1)S(1)}, u32[]{:S(2)}, u32[]{:S(2)}) async-start(bf16[64,4,5120]{2,1,0:T(4,128)(2,1)} %gather_fusion), calls=%async_computation | async-start | bytes 5242880 | tf_op jit(solution)/shard_map/all_to_all | solution.py:120
  31.7 0.7 all-gather.2.cloned.1.call-update
  32.5 3.1 %pad_maximum_fusion.1 = bf16[1024,1024]{1,0:T(8,128)(2,1)} fusion(bf16[1024,512]{1,0:T(8,128)(2,1)} %bitcast.121, bf16[1024,512]{1,0:T(8,128)(2,1)} %bitcast.119), kind=kLoop, calls=%fused_computation.5 | loop fusion | flops 4194304 | bytes 4194304 | tf_op jit(solution)/shard_map/concatenate | solution.py:145
  35.6 2.4 collective-permute-start
  38.7 0.6 reduce-window.18
  40.0 57.6 %all-to-all-done = bf16[64,4,5120]{2,1,0:T(4,128)(2,1)S(1)} async-done(((bf16[64,4,5120]{2,1,0:T(4,128)(2,1)}), bf16[64,4,5120]{2,1,0:T(4,128)(2,1)S(1)}, u32[]{:S(2)}, u32[]{:S(2)}) %all-to-all-start) | async-done | bytes 2621472 | tf_op jit(solution)/shard_map/all_to_all | solution.py:120
  97.6 2.7 gather_fusion.1
  100.3 2.5 reshape.543
  103.4 0.6 fusion.70
  104.4 52.7 %all-gather.2.cloned.1.call-done = bf16[1,1024,1024]{2,1,0:T(8,128)(2,1)} async-done(((bf16[1,16,1024]{2,1,0:T(8,128)(2,1)}), bf16[1,1024,1024]{2,1,0:T(8,128)(2,1)}) %all-gather.2.cloned.1.call-update) | async-done | bytes 2097168 | tf_op jit(solution)/shard_map/all_gather | solution.py:130
  157.1 2.2 multiply_reduce_fusion.1
  159.4 2.8 gather_fusion.2
  162.2 10.1 %all-to-all-start.1 = ((bf16[64,8,1024]{2,1,0:T(8,128)(2,1)}), bf16[64,8,1024]{2,1,0:T(8,128)(2,1)}, u32[]{:S(2)}, u32[]{:S(2)}) async-start(bf16[64,8,1024]{2,1,0:T(8,128)(2,1)} %bitcast.20), calls=%async_computation.1 | async-start | bytes 2097152 | tf_op jit(solution)/shard_map/all_to_all | solution.py:169
  172.2 2.6 collective-permute-start.1
  174.9 39.3 %collective-permute-done.1 = bf16[512,1024]{1,0:T(8,128)(2,1)} collective-permute-done((bf16[512,1024]{1,0:T(8,128)(2,1)S(1)}, bf16[512,1024]{1,0:T(8,128)(2,1)}, u32[]{:S(2)}, u32[]{:S(2)}) %collective-permute-start.1) | collective-permute-done | bytes 1048608 | tf_op jit(solution)/shard_map/ppermute | solution.py:10
  214.2 4.1 %maximum_select_fusion = bf16[1024,1024]{1,0:T(8,128)(2,1)} fusion(bf16[512,1024]{1,0:T(8,128)(2,1)S(1)} %bitcast.118, bf16[512,1024]{1,0:T(8,128)(2,1)} %collective-permute-done.1, pred[]{:T(512)S(6)} %eq.150), kind=kLoop, calls=%fused_computation.19 | loop fusion | flops 9437184 | bytes 4194305 | tf_op jit(solution)/shard_map/jit(_where)/select_n | solution.py:162
  218.3 3.1 %fusion.68 = (bf16[1024,512]{1,0:T(8,128)(2,1)}, bf16[1024,512]{1,0:T(8,128)(2,1)}) fusion(bf16[1024,1024]{1,0:T(8,128)(2,1)} %collective-permute-done), kind=kLoop, calls=%fused_computation.141 | loop fusion | bytes 4194304 | tf_op jit(solution)/shard_map/slice | solution.py:151
  221.3 3.3 %fusion.1 = f32[512,1024]{1,0:T(8,128)S(1)} fusion(bf16[1024,512]{1,0:T(8,128)(2,1)S(1)} %bitcast.120, bf16[1024,512]{1,0:T(8,128)(2,1)} %get-tuple-element.12, pred[]{:T(512)S(6)} %eq.150, bf16[64,8,1024]{2,1,0:T(8,128)(2,1)} %all-to-all-done.1), kind=kOutput, calls=%fused_computation.8 | convolution fusion | flops 1083179008 | bytes 5242881 | tf_op jit(solution)/shard_map/dot_general | solution.py:87
  224.7 3.8 %multiply_convert_fusion = bf16[512,1024]{1,0:T(8,128)(2,1)S(1)} fusion(f32[512,1024]{1,0:T(8,128)S(1)} %fusion.1, bf16[1024,512]{1,0:T(8,128)(2,1)S(1)} %bitcast.122, bf16[1024,512]{1,0:T(8,128)(2,1)S(1)} %copy-done.5, pred[]{:T(512)S(6)} %eq.150, bf16[64,8,1024]{2,1,0:T(8,128)(2,1)} %all-to-all-done.1), kind=kOutput, calls=%fused_computation.23 | convolution fusion | flops 1086324736 | bytes 6291457 | tf_op jit(solution)/shard_map/dot_general | solution.py:88
  228.4 0.7 convolution_convert_fusion.1
  229.2 1.7 fusion.18
  230.9 12.6 %all-to-all-start.2 = ((bf16[64,8,1024]{2,1,0:T(8,128)(2,1)}), bf16[64,8,1024]{2,1,0:T(8,128)(2,1)S(1)}, u32[]{:S(2)}, u32[]{:S(2)}) async-start(bf16[64,8,1024]{2,1,0:T(8,128)(2,1)} %fusion.18), calls=%async_computation.2 | async-start | bytes 2097152 | tf_op jit(solution)/shard_map/all_to_all | solution.py:171
  244.2 27.0 %all-to-all-done.2 = bf16[64,8,1024]{2,1,0:T(8,128)(2,1)S(1)} async-done(((bf16[64,8,1024]{2,1,0:T(8,128)(2,1)}), bf16[64,8,1024]{2,1,0:T(8,128)(2,1)S(1)}, u32[]{:S(2)}, u32[]{:S(2)}) %all-to-all-start.2) | async-done | bytes 1048608 | tf_op jit(solution)/shard_map/all_to_all | solution.py:171
  271.3 1.2 gather_fusion.3
  272.4 0.7 reshape.553
  273.1 1.3 multiply_reduce_fusion
  274.5 7.0 %collective-permute-done.2 = bf16[1,128,1024]{2,1,0:T(8,128)(2,1)S(1)} collective-permute-done((bf16[1,128,1024]{2,1,0:T(8,128)(2,1)S(1)}, bf16[1,128,1024]{2,1,0:T(8,128)(2,1)S(1)}, u32[]{:S(2)}, u32[]{:S(2)}) %collective-permute-start.2) | collective-permute-done | bytes 262176 | tf_op jit(solution)/shard_map/ppermute | solution.py:16
  281.5 0.7 copy.43
  (73 shorter events, 3.5 us)
Async XLA Ops:
  6.5 237.3 %copy-start = (bf16[1,1024,32]{1,2,0:T(8,128)(2,1)S(1)}, bf16[1,1024,32]{1,2,0:T(8,128)(2,1)}, u32[]{:S(2)}) copy-start(bf16[1,1024,32]{1,2,0:T(8,128)(2,1)} %param.16) | copy-start | bytes 196612
  15.1 82.5 %all-to-all-start = ((bf16[64,4,5120]{2,1,0:T(4,128)(2,1)}), bf16[64,4,5120]{2,1,0:T(4,128)(2,1)S(1)}, u32[]{:S(2)}, u32[]{:S(2)}) async-start(bf16[64,4,5120]{2,1,0:T(4,128)(2,1)} %gather_fusion), calls=%async_computation | async-start | bytes 5242880 | tf_op jit(solution)/shard_map/all_to_all | solution.py:120
  31.7 125.4 %all-gather.2.cloned.1.call-start = ((), (), s32[]{:S(2)}) async-start(), calls=%async_computation.3 | async-start | bytes 2129920 | tf_op jit(solution)/shard_map/all_gather | solution.py:130
  32.4 5.5 %copy-start.6 = (s32[1,128,2]{1,2,0:T(2,128)S(1)}, s32[1,128,2]{1,2,0:T(2,128)}, u32[]{:S(2)}) copy-start(s32[1,128,2]{1,2,0:T(2,128)} %param.14) | copy-start | bytes 3076
  32.4 5.9 %copy-start.8 = (s32[1,1,4]{2,1,0:T(1,128)S(1)}, s32[1,1,4]{2,1,0:T(1,128)}, u32[]{:S(2)}) copy-start(s32[1,1,4]{2,1,0:T(1,128)} %param.12) | copy-start | bytes 52
  32.4 6.1 %copy-start.9 = (s32[1,1,4]{2,1,0:T(1,128)S(1)}, s32[1,1,4]{2,1,0:T(1,128)}, u32[]{:S(2)}) copy-start(s32[1,1,4]{2,1,0:T(1,128)} %param.13) | copy-start | bytes 52
  32.5 7.1 %copy-start.7 = (s32[1,2,32]{2,1,0:T(2,128)S(1)}, s32[1,2,32]{2,1,0:T(2,128)}, u32[]{:S(2)}) copy-start(s32[1,2,32]{2,1,0:T(2,128)} %param.11) | copy-start | bytes 772
  35.6 182.7 %collective-permute-start = (bf16[1024,1024]{1,0:T(8,128)(2,1)}, bf16[1024,1024]{1,0:T(8,128)(2,1)}, u32[]{:S(2)}, u32[]{:S(2)}) collective-permute-start(bf16[1024,1024]{1,0:T(8,128)(2,1)} %pad_maximum_fusion.1), channel_id=1, source_target_pairs={{0,1},{1,0},{2,3},{3,2},{4,5},{5,4},{6,7},{7,6},{8,9},{9,8},{10,11... | collective-permute-start | bytes 6291464 | tf_op jit(solution)/shard_map/ppermute | solution.py:10
  162.2 10.1 %copy-start.2 = (bf16[1,512,1024]{2,1,0:T(8,128)(2,1)S(1)}, bf16[1,512,1024]{2,1,0:T(8,128)(2,1)}, u32[]{:S(2)}) copy-start(bf16[1,512,1024]{2,1,0:T(8,128)(2,1)} %param.19) | copy-start | bytes 3145732
  162.2 59.2 %all-to-all-start.1 = ((bf16[64,8,1024]{2,1,0:T(8,128)(2,1)}), bf16[64,8,1024]{2,1,0:T(8,128)(2,1)}, u32[]{:S(2)}, u32[]{:S(2)}) async-start(bf16[64,8,1024]{2,1,0:T(8,128)(2,1)} %bitcast.20), calls=%async_computation.1 | async-start | bytes 2097152 | tf_op jit(solution)/shard_map/all_to_all | solution.py:169
  172.2 41.9 %collective-permute-start.1 = (bf16[512,1024]{1,0:T(8,128)(2,1)S(1)}, bf16[512,1024]{1,0:T(8,128)(2,1)}, u32[]{:S(2)}, u32[]{:S(2)}) collective-permute-start(bf16[512,1024]{1,0:T(8,128)(2,1)S(1)} %bitcast.117), channel_id=1, source_target_pairs={{0,1},{1,0},{2,3},{3,2},{4,5},{5,4},{6,7},{7,6},{8,9},{9,8},{10,11... | collective-permute-start | bytes 3145736 | tf_op jit(solution)/shard_map/ppermute | solution.py:10
  218.3 3.1 %copy-start.3 = (bf16[1,1024,512]{2,1,0:T(8,128)(2,1)S(1)}, bf16[1,1024,512]{2,1,0:T(8,128)(2,1)}, u32[]{:S(2)}) copy-start(bf16[1,1024,512]{2,1,0:T(8,128)(2,1)} %param.17) | copy-start | bytes 3145732
  221.3 3.3 %copy-start.4 = (bf16[1,1024,512]{2,1,0:T(8,128)(2,1)S(1)}, bf16[1,1024,512]{2,1,0:T(8,128)(2,1)}, u32[]{:S(2)}) copy-start(bf16[1,1024,512]{2,1,0:T(8,128)(2,1)} %param.18) | copy-start | bytes 3145732
  221.3 3.3 %copy-start.5 = (bf16[1024,512]{1,0:T(8,128)(2,1)S(1)}, bf16[1024,512]{1,0:T(8,128)(2,1)}, u32[]{:S(2)}) copy-start(bf16[1024,512]{1,0:T(8,128)(2,1)} %get-tuple-element.11) | copy-start | bytes 3145732
  224.7 3.8 %copy-start.1 = (bf16[1024,1024]{1,0:T(8,128)(2,1)S(1)}, bf16[1024,1024]{1,0:T(8,128)(2,1)}, u32[]{:S(2)}) copy-start(bf16[1024,1024]{1,0:T(8,128)(2,1)} %maximum_select_fusion) | copy-start | bytes 6291460
  230.9 40.4 %all-to-all-start.2 = ((bf16[64,8,1024]{2,1,0:T(8,128)(2,1)}), bf16[64,8,1024]{2,1,0:T(8,128)(2,1)S(1)}, u32[]{:S(2)}, u32[]{:S(2)}) async-start(bf16[64,8,1024]{2,1,0:T(8,128)(2,1)} %fusion.18), calls=%async_computation.2 | async-start | bytes 2097152 | tf_op jit(solution)/shard_map/all_to_all | solution.py:171
  274.5 7.0 %collective-permute-start.2 = (bf16[1,128,1024]{2,1,0:T(8,128)(2,1)S(1)}, bf16[1,128,1024]{2,1,0:T(8,128)(2,1)S(1)}, u32[]{:S(2)}, u32[]{:S(2)}) collective-permute-start(bf16[1,128,1024]{2,1,0:T(8,128)(2,1)S(1)} %fusion.44), channel_id=1, source_target_pairs={{448,0},{0,64},{64,128},{128,192},{192,256},{256,320},{320,384},{3... | collective-permute-start | bytes 786440 | tf_op jit(solution)/shard_map/ppermute | solution.py:16
Sparse Core Ops, SparseCore 0:
  35.6 121.4 all-gather.1
where the time goes:
time: 290 us; the launch traced here: 289 us
  waiting for transfers between devices  184 us (63%)
  starting transfers between devices  44.3 us (15%)
  local copies, waits for them, and re-layouts  22.7 us (8%)
  between operations  13.8 us (5%)
  matrix products  12.5 us (4%)
  other arithmetic  11.4 us (4%)
    all_to_all x1, waiting for transfers between devices, shards(): lax.all_to_all(outgoing, 'expert', split_axis=0, concat_axis=0, tiled=True)  57.6 us
    all_gather x1, waiting for transfers between devices, shards(): lax.all_gather(out_proj, 'expert', axis=1, tiled=True)[0]  52.7 us
    ppermute x2, waiting for transfers between devices, swapped(): lax.ppermute(shard, axis, [(i, i ^ 1 << apart) for i in range(lax.axis_si...  39.3 us
    all_to_all x1, waiting for transfers between devices, shards(): lax.all_to_all(served, 'expert', split_axis=0, concat_axis=0, tiled=True)  27 us
    all_to_all x1, starting transfers between devices, shards(): lax.all_to_all(outgoing, 'expert', split_axis=0, concat_axis=0, tiled=True)  16.6 us
    all_to_all x1, starting transfers between devices, shards(): lax.all_to_all(served, 'expert', split_axis=0, concat_axis=0, tiled=True)  12.6 us
    all_to_all x1, starting transfers between devices, shards(): lax.all_to_all(sent_rows, 'expert', split_axis=0, concat_axis=0, tiled=True)  10.1 us
    ppermute x1, waiting for transfers between devices, from_behind(): return lax.ppermute(block, axis, route)  6.99 us
  transfers between devices with their start and end apart: 7, of which 5 were waited for; matrix products, arithmetic and copies ran while one was open for 9% of the time, Pallas kernels for 0%

commit v1 on v0

--- a/solution.py
+++ b/solution.py
@@ -127,7 +127,7 @@
     mixed_in = attend(balanced, user_pages[0, 0], tails[0, 0], page_rows)
     projected = jnp.dot(
         mixed_in,
-        lax.all_gather(out_proj, "expert", axis=1, tiled=True)[0],
+        jnp.concatenate(lax.all_gather(out_proj, "expert"), axis=1)[0],
         preferred_element_type=jnp.float32,
     )
     resid = (balanced[:, 4 * model_width :].astype(jnp.float32) + projected).astype(jnp.bfloat16)

time: 290 us -> 289 us (level)
  transfers between devices with their start and end apart: 7 -> 7, of which waited for: 5 -> 5; matrix products, arithmetic and copies ran while one was open for 9% -> 8% of each run, Pallas kernels for 0% -> 0%
where the time goes in v1:
time: 289 us
  waiting for transfers between devices  184 us (64%)
  starting transfers between devices  44.3 us (15%)
  local copies, waits for them, and re-layouts  22.7 us (8%)
  between operations  13.8 us (5%)
  matrix products  13 us (4%)
  other arithmetic  10.7 us (4%)
    all_to_all x1, waiting for transfers between devices, shards(): lax.all_to_all(outgoing, 'expert', split_axis=0, concat_axis=0, tiled=True)  57.5 us
    all_gather x1, waiting for transfers between devices, shards(): lax.all_gather(out_proj, 'expert')  52.7 us
    ppermute x2, waiting for transfers between devices, swapped(): lax.ppermute(shard, axis, [(i, i ^ 1 << apart) for i in range(lax.axis_si...  39.3 us
    all_to_all x1, waiting for transfers between devices, shards(): lax.all_to_all(served, 'expert', split_axis=0, concat_axis=0, tiled=True)  27 us
    all_to_all x1, starting transfers between devices, shards(): lax.all_to_all(outgoing, 'expert', split_axis=0, concat_axis=0, tiled=True)  16.6 us
    all_to_all x1, starting transfers between devices, shards(): lax.all_to_all(served, 'expert', split_axis=0, concat_axis=0, tiled=True)  12.6 us
    all_to_all x1, starting transfers between devices, shards(): lax.all_to_all(sent_rows, 'expert', split_axis=0, concat_axis=0, tiled=True)  10.1 us
    ppermute x1, waiting for transfers between devices, from_behind(): return lax.ppermute(block, axis, route)  6.99 us
  transfers between devices with their start and end apart: 7, of which 5 were waited for; matrix products, arithmetic and copies ran while one was open for 8% of the time, Pallas kernels for 0%

profile of v1, /device:TPU:8, one launch (start us, length us, event | category | flops | bytes accessed | tf_op | source)
XLA Modules:
  0.0 288.7 jit_solution(14095413754244489750)
XLA Ops:
  6.5 0.8 and_select_fusion.2
  7.3 0.7 slice_bitcast_fusion
  8.3 2.6 reshape_squeeze.6
  10.9 4.2 %gather_fusion = bf16[64,4,5120]{2,1,0:T(4,128)(2,1)} fusion(bf16[32,4,5120]{2,1,0:T(4,128)(2,1)S(1)} %reshape_squeeze.6, s32[1024]{0:T(1024)S(1)} %pad_clamp_fusion.3), kind=kCustom, calls=%fused_computation | custom fusion | bytes 5243136 | tf_op jit(solution)/shard_map/gather | solution.py:119
  15.0 16.6 %all-to-all-start = ((bf16[64,4,5120]{2,1,0:T(4,128)(2,1)}), bf16[64,4,5120]{2,1,0:T(4,128)(2,1)S(1)}, u32[]{:S(2)}, u32[]{:S(2)}) async-start(bf16[64,4,5120]{2,1,0:T(4,128)(2,1)} %gather_fusion), calls=%async_computation | async-start | bytes 5242880 | tf_op jit(solution)/shard_map/all_to_all | solution.py:120
  31.7 0.7 all-gather.3.cloned.1.call-update
  32.4 3.2 %pad_maximum_fusion.1 = bf16[1024,1024]{1,0:T(8,128)(2,1)} fusion(bf16[1024,512]{1,0:T(8,128)(2,1)} %bitcast.113, bf16[1024,512]{1,0:T(8,128)(2,1)} %bitcast.111), kind=kLoop, calls=%fused_computation.5 | loop fusion | flops 4194304 | bytes 4194304 | tf_op jit(solution)/shard_map/concatenate | solution.py:145
  35.6 2.4 collective-permute-start
  38.8 0.6 reduce-window.18
  40.1 57.5 %all-to-all-done = bf16[64,4,5120]{2,1,0:T(4,128)(2,1)S(1)} async-done(((bf16[64,4,5120]{2,1,0:T(4,128)(2,1)}), bf16[64,4,5120]{2,1,0:T(4,128)(2,1)S(1)}, u32[]{:S(2)}, u32[]{:S(2)}) %all-to-all-start) | async-done | bytes 2621472 | tf_op jit(solution)/shard_map/all_to_all | solution.py:120
  97.6 2.7 gather_fusion.1
  100.2 2.5 reshape.543
  103.3 0.6 fusion.61
  104.3 52.7 %all-gather.3.cloned.1.call-done = bf16[64,16,1024]{2,1,0:T(8,128)(2,1)} async-done(((bf16[1,16,1024]{2,1,0:T(8,128)(2,1)}), bf16[64,16,1024]{2,1,0:T(8,128)(2,1)}) %all-gather.3.cloned.1.call-update) | async-done | bytes 2097168 | tf_op jit(solution)/shard_map/all_gather | solution.py:130
  157.0 2.2 multiply_reduce_fusion.1
  159.3 2.8 gather_fusion.2
  162.1 10.1 %all-to-all-start.1 = ((bf16[64,8,1024]{2,1,0:T(8,128)(2,1)}), bf16[64,8,1024]{2,1,0:T(8,128)(2,1)}, u32[]{:S(2)}, u32[]{:S(2)}) async-start(bf16[64,8,1024]{2,1,0:T(8,128)(2,1)} %bitcast.20), calls=%async_computation.1 | async-start | bytes 2097152 | tf_op jit(solution)/shard_map/all_to_all | solution.py:169
  172.2 2.6 collective-permute-start.1
  174.8 39.3 %collective-permute-done.1 = bf16[512,1024]{1,0:T(8,128)(2,1)} collective-permute-done((bf16[512,1024]{1,0:T(8,128)(2,1)S(1)}, bf16[512,1024]{1,0:T(8,128)(2,1)}, u32[]{:S(2)}, u32[]{:S(2)}) %collective-permute-start.1) | collective-permute-done | bytes 1048608 | tf_op jit(solution)/shard_map/ppermute | solution.py:10
  214.1 3.3 %maximum_select_fusion = bf16[1024,1024]{1,0:T(8,128)(2,1)S(1)} fusion(bf16[512,1024]{1,0:T(8,128)(2,1)} %bitcast.109, bf16[512,1024]{1,0:T(8,128)(2,1)} %collective-permute-done.1, pred[]{:T(512)S(6)} %eq.150), kind=kLoop, calls=%fused_computation.19 | loop fusion | flops 9437184 | bytes 4194305 | tf_op jit(solution)/shard_map/jit(_where)/select_n | solution.py:162
  217.4 3.1 %fusion.59 = (bf16[1024,512]{1,0:T(8,128)(2,1)}, bf16[1024,512]{1,0:T(8,128)(2,1)}) fusion(bf16[1024,1024]{1,0:T(8,128)(2,1)} %collective-permute-done), kind=kLoop, calls=%fused_computation.139 | loop fusion | bytes 4194304 | tf_op jit(solution)/shard_map/slice | solution.py:151
  220.5 3.9 %fusion.1 = f32[512,1024]{1,0:T(8,128)S(1)} fusion(bf16[1024,512]{1,0:T(8,128)(2,1)} %bitcast.112, bf16[1024,512]{1,0:T(8,128)(2,1)} %get-tuple-element.12, pred[]{:T(512)S(6)} %eq.150, bf16[64,8,1024]{2,1,0:T(8,128)(2,1)} %all-to-all-done.1), kind=kOutput, calls=%fused_computation.8 | convolution fusion | flops 1083179008 | bytes 5242881 | tf_op jit(solution)/shard_map/dot_general | solution.py:87
  224.4 3.6 %multiply_convert_fusion = bf16[512,1024]{1,0:T(8,128)(2,1)S(1)} fusion(f32[512,1024]{1,0:T(8,128)S(1)} %fusion.1, bf16[1024,512]{1,0:T(8,128)(2,1)S(1)} %bitcast.114, bf16[1024,512]{1,0:T(8,128)(2,1)S(1)} %copy-done.3, pred[]{:T(512)S(6)} %eq.150, bf16[64,8,1024]{2,1,0:T(8,128)(2,1)} %all-to-all-done.1), kind=kOutput, calls=%fused_computation.21 | convolution fusion | flops 1086324736 | bytes 6291457 | tf_op jit(solution)/shard_map/dot_general | solution.py:88
  228.0 0.7 convolution_convert_fusion.1
  228.8 1.7 fusion.16
  230.5 12.6 %all-to-all-start.2 = ((bf16[64,8,1024]{2,1,0:T(8,128)(2,1)}), bf16[64,8,1024]{2,1,0:T(8,128)(2,1)S(1)}, u32[]{:S(2)}, u32[]{:S(2)}) async-start(bf16[64,8,1024]{2,1,0:T(8,128)(2,1)} %fusion.16), calls=%async_computation.2 | async-start | bytes 2097152 | tf_op jit(solution)/shard_map/all_to_all | solution.py:171
  243.8 27.0 %all-to-all-done.2 = bf16[64,8,1024]{2,1,0:T(8,128)(2,1)S(1)} async-done(((bf16[64,8,1024]{2,1,0:T(8,128)(2,1)}), bf16[64,8,1024]{2,1,0:T(8,128)(2,1)S(1)}, u32[]{:S(2)}, u32[]{:S(2)}) %all-to-all-start.2) | async-done | bytes 1048608 | tf_op jit(solution)/shard_map/all_to_all | solution.py:171
  270.8 1.2 gather_fusion.3
  272.0 0.7 reshape.553
  272.7 1.3 multiply_reduce_fusion
  274.1 7.0 %collective-permute-done.2 = bf16[1,128,1024]{2,1,0:T(8,128)(2,1)S(1)} collective-permute-done((bf16[1,128,1024]{2,1,0:T(8,128)(2,1)S(1)}, bf16[1,128,1024]{2,1,0:T(8,128)(2,1)S(1)}, u32[]{:S(2)}, u32[]{:S(2)}) %collective-permute-start.2) | collective-permute-done | bytes 262176 | tf_op jit(solution)/shard_map/ppermute | solution.py:16
  281.1 0.7 copy.55
  (69 shorter events, 3.5 us)
Async XLA Ops:
  6.5 236.9 %copy-start = (bf16[1,1024,32]{1,2,0:T(8,128)(2,1)S(1)}, bf16[1,1024,32]{1,2,0:T(8,128)(2,1)}, u32[]{:S(2)}) copy-start(bf16[1,1024,32]{1,2,0:T(8,128)(2,1)} %param.16) | copy-start | bytes 196612
  15.0 82.5 %all-to-all-start = ((bf16[64,4,5120]{2,1,0:T(4,128)(2,1)}), bf16[64,4,5120]{2,1,0:T(4,128)(2,1)S(1)}, u32[]{:S(2)}, u32[]{:S(2)}) async-start(bf16[64,4,5120]{2,1,0:T(4,128)(2,1)} %gather_fusion), calls=%async_computation | async-start | bytes 5242880 | tf_op jit(solution)/shard_map/all_to_all | solution.py:120
  31.6 125.4 %all-gather.3.cloned.1.call-start = ((), (), s32[]{:S(2)}) async-start(), calls=%async_computation.3 | async-start | bytes 2129920 | tf_op jit(solution)/shard_map/all_gather | solution.py:130
  32.4 5.6 %copy-start.4 = (s32[1,128,2]{1,2,0:T(2,128)S(1)}, s32[1,128,2]{1,2,0:T(2,128)}, u32[]{:S(2)}) copy-start(s32[1,128,2]{1,2,0:T(2,128)} %param.14) | copy-start | bytes 3076
  32.4 6.0 %copy-start.6 = (s32[1,1,4]{2,1,0:T(1,128)S(1)}, s32[1,1,4]{2,1,0:T(1,128)}, u32[]{:S(2)}) copy-start(s32[1,1,4]{2,1,0:T(1,128)} %param.12) | copy-start | bytes 52
  32.4 6.2 %copy-start.7 = (s32[1,1,4]{2,1,0:T(1,128)S(1)}, s32[1,1,4]{2,1,0:T(1,128)}, u32[]{:S(2)}) copy-start(s32[1,1,4]{2,1,0:T(1,128)} %param.13) | copy-start | bytes 52
  32.4 7.2 %copy-start.5 = (s32[1,2,32]{2,1,0:T(2,128)S(1)}, s32[1,2,32]{2,1,0:T(2,128)}, u32[]{:S(2)}) copy-start(s32[1,2,32]{2,1,0:T(2,128)} %param.11) | copy-start | bytes 772
  35.6 181.8 %collective-permute-start = (bf16[1024,1024]{1,0:T(8,128)(2,1)}, bf16[1024,1024]{1,0:T(8,128)(2,1)}, u32[]{:S(2)}, u32[]{:S(2)}) collective-permute-start(bf16[1024,1024]{1,0:T(8,128)(2,1)} %pad_maximum_fusion.1), channel_id=1, source_target_pairs={{0,1},{1,0},{2,3},{3,2},{4,5},{5,4},{6,7},{7,6},{8,9},{9,8},{10,11... | collective-permute-start | bytes 6291464 | tf_op jit(solution)/shard_map/ppermute | solution.py:10
  162.1 10.1 %copy-start.1 = (bf16[1,512,1024]{2,1,0:T(8,128)(2,1)S(1)}, bf16[1,512,1024]{2,1,0:T(8,128)(2,1)}, u32[]{:S(2)}) copy-start(bf16[1,512,1024]{2,1,0:T(8,128)(2,1)} %param.19) | copy-start | bytes 3145732
  162.1 58.3 %all-to-all-start.1 = ((bf16[64,8,1024]{2,1,0:T(8,128)(2,1)}), bf16[64,8,1024]{2,1,0:T(8,128)(2,1)}, u32[]{:S(2)}, u32[]{:S(2)}) async-start(bf16[64,8,1024]{2,1,0:T(8,128)(2,1)} %bitcast.20), calls=%async_computation.1 | async-start | bytes 2097152 | tf_op jit(solution)/shard_map/all_to_all | solution.py:169
  172.2 41.9 %collective-permute-start.1 = (bf16[512,1024]{1,0:T(8,128)(2,1)S(1)}, bf16[512,1024]{1,0:T(8,128)(2,1)}, u32[]{:S(2)}, u32[]{:S(2)}) collective-permute-start(bf16[512,1024]{1,0:T(8,128)(2,1)S(1)} %bitcast.110), channel_id=1, source_target_pairs={{0,1},{1,0},{2,3},{3,2},{4,5},{5,4},{6,7},{7,6},{8,9},{9,8},{10,11... | collective-permute-start | bytes 3145736 | tf_op jit(solution)/shard_map/ppermute | solution.py:10
  220.5 3.9 %copy-start.2 = (bf16[1,1024,512]{2,1,0:T(8,128)(2,1)S(1)}, bf16[1,1024,512]{2,1,0:T(8,128)(2,1)}, u32[]{:S(2)}) copy-start(bf16[1,1024,512]{2,1,0:T(8,128)(2,1)} %param.18) | copy-start | bytes 3145732
  220.5 3.9 %copy-start.3 = (bf16[1024,512]{1,0:T(8,128)(2,1)S(1)}, bf16[1024,512]{1,0:T(8,128)(2,1)}, u32[]{:S(2)}) copy-start(bf16[1024,512]{1,0:T(8,128)(2,1)} %get-tuple-element.11) | copy-start | bytes 3145732
  230.5 40.4 %all-to-all-start.2 = ((bf16[64,8,1024]{2,1,0:T(8,128)(2,1)}), bf16[64,8,1024]{2,1,0:T(8,128)(2,1)S(1)}, u32[]{:S(2)}, u32[]{:S(2)}) async-start(bf16[64,8,1024]{2,1,0:T(8,128)(2,1)} %fusion.16), calls=%async_computation.2 | async-start | bytes 2097152 | tf_op jit(solution)/shard_map/all_to_all | solution.py:171
  274.1 7.0 %collective-permute-start.2 = (bf16[1,128,1024]{2,1,0:T(8,128)(2,1)S(1)}, bf16[1,128,1024]{2,1,0:T(8,128)(2,1)S(1)}, u32[]{:S(2)}, u32[]{:S(2)}) collective-permute-start(bf16[1,128,1024]{2,1,0:T(8,128)(2,1)S(1)} %fusion.35), channel_id=1, source_target_pairs={{448,0},{0,64},{64,128},{128,192},{192,256},{256,320},{320,384},{3... | collective-permute-start | bytes 786440 | tf_op jit(solution)/shard_map/ppermute | solution.py:16
Sparse Core Ops, SparseCore 0:
  35.5 121.4 all-gather.2
